TPU v7x, 32 devices: a whole 2x2x4 slice. The times are simulated.
32 devices in a mesh: fsdp: 4 (over y, x), heads: 2 (over core), tensor: 4 (over z).
Axes of the slice: x: 2, y: 2, z: 4, core: 2. Of those that a mesh axis runs over, the one named last changes fastest.
Arguments:
- inputs: float32 [32, 729, 1152], P(('fsdp', 'heads', 'tensor')), may hold values from -6 to 6
- cotangent: float32 [32, 729, 1152], P(('fsdp', 'heads', 'tensor')), may hold values from -6 to 6
- image_adapter_index: int32 [32], replicated, may hold values from 0 to 7
- first_norm_gain: float32 [1152], replicated, may hold values from 0.5 to 1.5
- first_norm_bias: float32 [1152], replicated, may hold values from -3 to 3
- second_norm_gain: float32 [1152], replicated, may hold values from 0.5 to 1.5
- second_norm_bias: float32 [1152], replicated, may hold values from -3 to 3
- query_key_value_weight: bfloat16 [1152, 3, 1152], P('fsdp', None, 'heads'), may hold values from -0.1875 to 0.1875
- attention_output_weight: bfloat16 [1152, 1152], P('fsdp', 'heads'), may hold values from -3 to 3
- up_weight: bfloat16 [1152, 4304], P('fsdp', 'tensor'), may hold values from -0.1875 to 0.1875
- down_weight: bfloat16 [1152, 4304], P('fsdp', 'tensor'), may hold values from -0.09375 to 0.09375
- up_projection_bias: bfloat16 [4304], P('tensor'), may hold values from -3 to 3
- down_projection_bias: bfloat16 [1152], replicated, may hold values from -3 to 3
- query_key_value_adapter_first: bfloat16 [3, 8, 1152, 16], replicated, may hold values from -0.1875 to 0.1875
- query_key_value_adapter_second: bfloat16 [3, 8, 16, 1152], P(None, None, None, 'heads'), may hold values from -0.75 to 0.75
- projection_adapter_first: bfloat16 [8, 1152, 16], P(None, 'heads'), may hold values from -3 to 3
- projection_adapter_second: bfloat16 [8, 16, 1152], replicated, may hold values from -0.75 to 0.75
- up_adapter_first: bfloat16 [8, 1152, 16], replicated, may hold values from -0.1875 to 0.1875
- up_adapter_second: bfloat16 [8, 16, 4304], P(None, None, 'tensor'), may hold values from -0.75 to 0.75
- down_adapter_first: bfloat16 [8, 16, 4304], P(None, None, 'tensor'), may hold values from -0.09375 to 0.09375
- down_adapter_second: bfloat16 [8, 16, 1152], replicated, may hold values from -0.75 to 0.75
Outputs:
- layer_output: float32 [32, 729, 1152], P(('fsdp', 'heads', 'tensor'))
- grad_input: float32 [32, 729, 1152], P(('fsdp', 'heads', 'tensor'))
- grad_qkv_in: float32 [3, 8, 1152, 16], replicated
- grad_qkv_out: float32 [3, 8, 16, 1152], P(None, None, None, 'heads')
- grad_proj_in: float32 [8, 1152, 16], P(None, 'heads')
- grad_proj_out: float32 [8, 16, 1152], replicated
- grad_up_in: float32 [8, 1152, 16], replicated
- grad_up_out: float32 [8, 16, 4304], P(None, None, 'tensor')
- grad_down_in: float32 [8, 16, 4304], P(None, None, 'tensor')
- grad_down_out: float32 [8, 16, 1152], replicated
All inputs are finite; a program needn't handle non-finite values.
Results may differ from a plain program's by a relative error of at most 0.02.
Values may be sent and summed in bfloat16 or wider, within the bound.
A program may use at most 256 MiB of HBM per device.

v0:
```python
import jax
import jax.numpy as jnp
from jax import lax
from jax.sharding import PartitionSpec as P

HEAD_DIM = 72
highest_precision = lax.Precision.HIGHEST
norm_eps = 1e-06


def normalize(values, gain, bias):
    mean = jnp.mean(values, axis=-1, keepdims=True)
    centred = values - mean
    inverse = lax.rsqrt(jnp.mean(centred * centred, axis=-1, keepdims=True) + norm_eps)
    unit = centred * inverse
    return (unit * gain + bias, unit, inverse)


def normalize_back(grad_norm, unit, inverse, gain):
    scaled = grad_norm * gain
    return inverse * (
        scaled
        - jnp.mean(scaled, axis=-1, keepdims=True)
        - unit * jnp.mean(scaled * unit, axis=-1, keepdims=True)
    )


def gelu_tanh(values):
    return jax.nn.gelu(values, approximate=True)


def one_hot(ids, count):
    return (ids[:, None] == jnp.arange(count, dtype=jnp.int32)[None, :]).astype(jnp.float32)


def by_adapter(hot, per_image):
    return jnp.einsum("ia,ixy->axy", hot, per_image, precision=highest_precision)


def attend_forward(operands):
    query, keyed, valued = operands
    scores = jnp.einsum(
        "qhd,khd->hqk", query, keyed, preferred_element_type=jnp.float32
    ) * HEAD_DIM ** (-0.5)
    top = jnp.max(scores, axis=-1, keepdims=True)
    weights = jnp.exp(scores - top)
    total = jnp.sum(weights, axis=-1, keepdims=True)
    probs = (weights / total).astype(jnp.bfloat16)
    mixed_heads = jnp.einsum("hqk,khd->qhd", probs, valued, preferred_element_type=jnp.float32)
    return (mixed_heads.astype(jnp.bfloat16), (top + jnp.log(total))[..., 0])


def attend_back(operands):
    query, keyed, valued, grad_mixed, log_total = operands
    scale = HEAD_DIM ** (-0.5)
    scores = jnp.einsum("qhd,khd->hqk", query, keyed, preferred_element_type=jnp.float32) * scale
    probs = jnp.exp(scores - log_total[..., None])
    grad_probs = jnp.einsum("qhd,khd->hqk", grad_mixed, valued, preferred_element_type=jnp.float32)
    grad_values = jnp.einsum(
        "hqk,qhd->khd", probs.astype(jnp.bfloat16), grad_mixed, preferred_element_type=jnp.float32
    )
    inner = jnp.sum(probs * grad_probs, axis=-1, keepdims=True)
    grad_scores = (probs * (grad_probs - inner)).astype(jnp.bfloat16)
    grad_query = (
        jnp.einsum("hqk,khd->qhd", grad_scores, keyed, preferred_element_type=jnp.float32) * scale
    )
    grad_keys = (
        jnp.einsum("hqk,qhd->khd", grad_scores, query, preferred_element_type=jnp.float32) * scale
    )
    return (grad_query, grad_keys, grad_values)


def per_device(
    inputs,
    cotangent,
    image_adapter_index,
    first_norm_gain,
    first_norm_bias,
    second_norm_gain,
    second_norm_bias,
    query_key_value_weight,
    attention_output_weight,
    up_weight,
    down_weight,
    up_projection_bias,
    down_projection_bias,
    query_key_value_adapter_first,
    query_key_value_adapter_second,
    projection_adapter_first,
    projection_adapter_second,
    up_adapter_first,
    up_adapter_second,
    down_adapter_first,
    down_adapter_second,
):
    head_count = lax.axis_size("heads")
    unit_count = lax.axis_size("tensor")
    fsdp_index = lax.axis_index("fsdp")
    head_index = lax.axis_index("heads")
    unit_index = lax.axis_index("tensor")
    images, length, width = inputs.shape
    adapter_factors = query_key_value_adapter_first.shape[1]
    local = jnp.arange(images, dtype=jnp.int32)
    group = fsdp_index * head_count
    own_rows = ((group + head_index) * unit_count + unit_index) * images + local
    head_rows = (
        ((group + jnp.arange(head_count, dtype=jnp.int32))[:, None] * unit_count + unit_index)
        * images
        + local[None, :]
    ).reshape(-1)
    unit_rows = (
        ((group + head_index) * unit_count + jnp.arange(unit_count, dtype=jnp.int32))[:, None]
        * images
        + local[None, :]
    ).reshape(-1)
    owned_numbers = image_adapter_index[own_rows]
    head_numbers = image_adapter_index[head_rows]
    unit_numbers = image_adapter_index[unit_rows]
    query_key_value_whole, output_whole_weight, up_rows, down_rows = (
        lax.all_gather(query_key_value_weight, "fsdp", axis=0, tiled=True),
        lax.all_gather(attention_output_weight, "fsdp", axis=0, tiled=True),
        lax.all_gather(up_weight, "fsdp", axis=0, tiled=True),
        lax.all_gather(down_weight, "fsdp", axis=0, tiled=True),
    )
    norm1, unit1, inverse1 = normalize(inputs, first_norm_gain, first_norm_bias)
    ln1_all = lax.all_gather(norm1.astype(jnp.bfloat16), "heads", axis=0, tiled=True)
    (
        query_key_value_attention,
        output_attention_part,
        query_key_value_output_weight,
        projection_input_weight,
    ) = (
        query_key_value_whole,
        output_whole_weight,
        query_key_value_adapter_second,
        projection_adapter_first,
    )
    seen = ln1_all.shape[0]
    query_key_value_input_selected = query_key_value_adapter_first[:, head_numbers]
    qkv_out_sel = query_key_value_output_weight[:, head_numbers]
    query_key_value_middle = jnp.einsum(
        "obl,holm->hobm",
        ln1_all,
        query_key_value_input_selected,
        preferred_element_type=jnp.float32,
    )
    projected = jnp.einsum(
        "isd,djf->jisf", ln1_all, query_key_value_attention, preferred_element_type=jnp.float32
    )
    projected = projected + jnp.einsum(
        "klty,klye->klte",
        query_key_value_middle,
        qkv_out_sel.astype(jnp.float32),
        precision=highest_precision,
    )
    proj_low = projected.astype(jnp.bfloat16)
    local_width = proj_low.shape[-1]
    heads_local = local_width // HEAD_DIM
    shaped = proj_low.reshape(3, seen, length, heads_local, HEAD_DIM)
    mixed_heads, log_total = lax.map(attend_forward, (shaped[0], shaped[1], shaped[2]))
    mixed_heads = mixed_heads.reshape(seen, length, local_width)
    proj_in_sel = projection_input_weight[head_numbers]
    projection_output_selected = projection_adapter_second[head_numbers]
    projection_adapter_middle = jnp.einsum(
        "lby,lyg->lbg", mixed_heads, proj_in_sel, preferred_element_type=jnp.float32
    )
    attention_branch = jnp.einsum(
        "ise,de->isd", mixed_heads, output_attention_part, preferred_element_type=jnp.float32
    )
    attention_branch = attention_branch + jnp.einsum(
        "cmt,ctf->cmf",
        projection_adapter_middle,
        projection_output_selected.astype(jnp.float32),
        precision=highest_precision,
    )
    hidden = inputs + lax.psum_scatter(
        attention_branch.astype(jnp.bfloat16), "heads", scatter_dimension=0, tiled=True
    ).astype(jnp.float32)
    norm2, unit2, inverse2 = normalize(hidden, second_norm_gain, second_norm_bias)
    second_norm_reduced = norm2.astype(jnp.bfloat16)
    up_adapter_middle = jnp.einsum(
        "ego,eoh->egh",
        second_norm_reduced,
        up_adapter_first[owned_numbers],
        preferred_element_type=jnp.float32,
    ).astype(jnp.bfloat16)
    ln2_in, up_mid_in = (
        lax.all_gather(second_norm_reduced, "tensor", axis=0, tiled=True),
        lax.all_gather(up_adapter_middle, "tensor", axis=0, tiled=True),
    )
    up_cols, down_cols, bias_cols = (up_rows, down_rows, up_projection_bias)
    up_output_columns, down_input_columns = (up_adapter_second, down_adapter_first)
    up_input_selected = up_adapter_first[unit_numbers]
    up_out_sel = up_output_columns[unit_numbers]
    down_in_sel = down_input_columns[unit_numbers]
    down_output_selected = down_adapter_second[unit_numbers]
    residual_before = jnp.einsum(
        "isd,df->isf", ln2_in, up_cols, preferred_element_type=jnp.float32
    ) + bias_cols.astype(jnp.float32)
    residual_before = residual_before + jnp.einsum(
        "cbd,cdp->cbp",
        up_mid_in.astype(jnp.float32),
        up_out_sel.astype(jnp.float32),
        precision=highest_precision,
    )
    act_low = gelu_tanh(residual_before).astype(jnp.bfloat16)
    down_adapter_middle = jnp.einsum(
        "pco,pqo->pcq", act_low, down_in_sel, preferred_element_type=jnp.float32
    )
    mlp_part = jnp.einsum("isf,df->isd", act_low, down_cols, preferred_element_type=jnp.float32)
    mlp_part = mlp_part + jnp.einsum(
        "cmt,ctf->cmf",
        down_adapter_middle,
        down_output_selected.astype(jnp.float32),
        precision=highest_precision,
    )
    mlp_sum = lax.psum_scatter(
        mlp_part.astype(jnp.bfloat16), "tensor", scatter_dimension=0, tiled=True
    ).astype(jnp.float32)
    layer_output = hidden + mlp_sum + down_projection_bias.astype(jnp.float32)
    grad_mlp = cotangent.astype(jnp.bfloat16)
    grad_mlp_in = lax.all_gather(grad_mlp, "tensor", axis=0, tiled=True)
    grad_down_mid = jnp.einsum(
        "isd,ird->isr", grad_mlp_in, down_output_selected, preferred_element_type=jnp.float32
    )
    grad_act = jnp.einsum("isd,df->isf", grad_mlp_in, down_cols, preferred_element_type=jnp.float32)
    grad_act = grad_act + jnp.einsum(
        "cbd,cdp->cbp", grad_down_mid, down_in_sel.astype(jnp.float32), precision=highest_precision
    )
    ignored, gelu_pull = jax.vjp(gelu_tanh, residual_before)
    grad_before = gelu_pull(grad_act)[0].astype(jnp.bfloat16)
    grad_up_mid = jnp.einsum(
        "pco,pqo->pcq", grad_before, up_out_sel, preferred_element_type=jnp.float32
    )
    grad_ln2 = jnp.einsum("isf,df->isd", grad_before, up_cols, preferred_element_type=jnp.float32)
    grad_ln2 = grad_ln2 + jnp.einsum(
        "isr,idr->isd",
        grad_up_mid,
        up_input_selected.astype(jnp.float32),
        precision=highest_precision,
    )
    grad_ln2 = lax.psum_scatter(
        grad_ln2.astype(jnp.bfloat16), "tensor", scatter_dimension=0, tiled=True
    ).astype(jnp.float32)
    grad_hidden = cotangent + normalize_back(grad_ln2, unit2, inverse2, second_norm_gain)
    mlp_hot = one_hot(unit_numbers, adapter_factors)
    grad_up_in_part = by_adapter(
        mlp_hot, jnp.einsum("isd,isr->idr", ln2_in, grad_up_mid, precision=highest_precision)
    )
    grad_up_out_part = by_adapter(
        mlp_hot,
        jnp.einsum("isr,isf->irf", up_mid_in, grad_before, preferred_element_type=jnp.float32),
    )
    grad_down_in_part = by_adapter(
        mlp_hot, jnp.einsum("isr,isf->irf", grad_down_mid, act_low, precision=highest_precision)
    )
    grad_down_out_part = by_adapter(
        mlp_hot,
        jnp.einsum("isr,isd->ird", down_adapter_middle, grad_mlp_in, precision=highest_precision),
    )
    grad_branch = lax.all_gather(grad_hidden.astype(jnp.bfloat16), "heads", axis=0, tiled=True)
    grad_proj_mid = jnp.einsum(
        "isd,ird->isr", grad_branch, projection_output_selected, preferred_element_type=jnp.float32
    )
    grad_mixed = jnp.einsum(
        "isd,de->ise", grad_branch, output_attention_part, preferred_element_type=jnp.float32
    )
    grad_mixed = grad_mixed + jnp.einsum(
        "isr,ier->ise", grad_proj_mid, proj_in_sel.astype(jnp.float32), precision=highest_precision
    )
    grad_mixed = grad_mixed.astype(jnp.bfloat16).reshape(seen, length, heads_local, HEAD_DIM)
    grad_query, grad_keys, grad_values = lax.map(
        attend_back, (shaped[0], shaped[1], shaped[2], grad_mixed, log_total)
    )
    grad_proj = (
        jnp.stack([grad_query, grad_keys, grad_values])
        .reshape(3, seen, length, local_width)
        .astype(jnp.bfloat16)
    )
    grad_qkv_mid = jnp.einsum(
        "jisf,jirf->jisr", grad_proj, qkv_out_sel, preferred_element_type=jnp.float32
    )
    grad_ln1 = jnp.einsum(
        "jisf,djf->isd", grad_proj, query_key_value_attention, preferred_element_type=jnp.float32
    )
    grad_ln1 = grad_ln1 + jnp.einsum(
        "jisr,jidr->isd",
        grad_qkv_mid,
        query_key_value_input_selected.astype(jnp.float32),
        precision=highest_precision,
    )
    grad_ln1 = lax.psum_scatter(
        grad_ln1.astype(jnp.bfloat16), "heads", scatter_dimension=0, tiled=True
    ).astype(jnp.float32)
    grad_input = grad_hidden + normalize_back(grad_ln1, unit1, inverse1, first_norm_gain)
    attn_hot = one_hot(head_numbers, adapter_factors)
    qkv_in_image = jnp.einsum("isd,jisr->jidr", ln1_all, grad_qkv_mid, precision=highest_precision)
    grad_qkv_in_part = jnp.einsum(
        "ia,jidr->jadr", attn_hot, qkv_in_image, precision=highest_precision
    )
    qkv_out_image = jnp.einsum(
        "jisr,jisf->jirf", query_key_value_middle, grad_proj, precision=highest_precision
    )
    grad_qkv_out_part = jnp.einsum(
        "ia,jirf->jarf", attn_hot, qkv_out_image, precision=highest_precision
    )
    grad_proj_in_part = by_adapter(
        attn_hot,
        jnp.einsum("ise,isr->ier", mixed_heads, grad_proj_mid, precision=highest_precision),
    )
    grad_proj_out_part = by_adapter(
        attn_hot,
        jnp.einsum(
            "isr,isd->ird", projection_adapter_middle, grad_branch, precision=highest_precision
        ),
    )
    grad_qkv_in, grad_proj_out, grad_up_in, grad_down_out = lax.psum(
        (grad_qkv_in_part, grad_proj_out_part, grad_up_in_part, grad_down_out_part),
        ("fsdp", "heads", "tensor"),
    )
    grad_qkv_out, grad_proj_in = lax.psum(
        (grad_qkv_out_part, grad_proj_in_part), ("fsdp", "tensor")
    )
    grad_up_out, grad_down_in = (
        lax.psum(grad_up_out_part.astype(jnp.bfloat16), ("fsdp", "heads")).astype(jnp.float32),
        lax.psum(grad_down_in_part.astype(jnp.bfloat16), ("fsdp", "heads")).astype(jnp.float32),
    )
    return (
        layer_output,
        grad_input,
        grad_qkv_in,
        grad_qkv_out,
        grad_proj_in,
        grad_proj_out,
        grad_up_in,
        grad_up_out,
        grad_down_in,
        grad_down_out,
    )


def solution(mesh):
    in_specs = (
        P(("fsdp", "heads", "tensor"), None, None),
        P(("fsdp", "heads", "tensor"), None, None),
        P(),
        P(),
        P(),
        P(),
        P(),
        P("fsdp", None, "heads"),
        P("fsdp", "heads"),
        P("fsdp", "tensor"),
        P("fsdp", "tensor"),
        P("tensor"),
        P(),
        P(),
        P(None, None, None, "heads"),
        P(None, "heads", None),
        P(),
        P(),
        P(None, None, "tensor"),
        P(None, None, "tensor"),
        P(),
    )
    out_specs = (
        P(("fsdp", "heads", "tensor"), None, None),
        P(("fsdp", "heads", "tensor"), None, None),
        P(),
        P(None, None, None, "heads"),
        P(None, "heads", None),
        P(),
        P(),
        P(None, None, "tensor"),
        P(None, None, "tensor"),
        P(),
    )
    return jax.shard_map(
        per_device, mesh=mesh, in_specs=in_specs, out_specs=out_specs, check_vma=False
    )
```

profile of v0, /device:TPU:0, one launch (start us, length us, event | category | flops | bytes accessed | tf_op | source)
XLA Modules:
  0.0 1267.5 jit_solution(7760785568148674721)
XLA Ops:
  36.3 54.6 %all-gather.13.cloned.1.call-done = bf16[1152,3,576]{2,0,1:T(8,128)(2,1)} async-done(((bf16[288,3,576]{2,0,1:T(8,128)(2,1)}), bf16[1152,3,576]{2,0,1:T(8,128)(2,1)}) %all-gather.13.cloned.1.call-update) | async-done | bytes 3981328 | tf_op jit(solution)/shard_map/all_gather | solution.py:120
  90.9 10.7 fusion.59
  109.1 57.2 %while.28 = (s32[]{:T(128)}, bf16[2,729,8,72]{1,3,2,0:T(8,128)(2,1)}, f32[2,8,729]{2,1,0:T(8,128)S(1)}, bf16[2,729,8,72]{1,3,2,0:T(8,128)(2,1)}, bf16[2,729,8,72...) while((s32[]{:T(128)}, bf16[2,729,8,72]{1,3,2,0:T(8,128)(2,1)}, ...), condition=%wide.region_5.6_spmd, body=%wide.region_2.5_spmd.sunk | while | flops 1263117824 | bytes 55831608 | solution.py:160
  109.1 9.9 multiply_reduce_fusion.8
  119.0 9.2 fusion.206
  128.2 9.3 fusion.207
  137.5 9.9 multiply_reduce_fusion.8
  156.6 9.3 fusion.207
  202.4 102.8 %all-gather.23.cloned.1.call-done = bf16[4,729,1152]{2,1,0:T(8,128)(2,1)} async-done(((bf16[1,729,1152]{2,1,0:T(8,128)(2,1)}), bf16[4,729,1152]{2,1,0:T(8,128)(2,1)}) %all-gather.23.cloned.1.call-update) | async-done | bytes 6718480 | tf_op jit(solution)/shard_map/all_gather | solution.py:222
  310.0 34.9 %all-gather.21.cloned.1.call-done = bf16[1152,1076]{1,0:T(8,128)(2,1)} async-done(((bf16[288,1076]{1,0:T(8,128)(2,1)}), bf16[1152,1076]{1,0:T(8,128)(2,1)}) %all-gather.21.cloned.1.call-update) | async-done | bytes 2479120 | tf_op jit(solution)/shard_map/all_gather | solution.py:123
  344.9 14.5 %fusion.69 = f32[4,729,1076]{1,2,0:T(8,128)} fusion(bf16[4,729,1152]{2,1,0:T(8,128)(2,1)} %all-gather.23.cloned.1.call-done, bf16[1152,1076]{1,0:T(8,128)(2,1)} %all-gather.21.cloned.1.call-done), kind=kOutput, calls=%fused_computation.114 | convolution fusion | flops 7229067264 | bytes 21748032 | tf_op jit(solution)/shard_map/isd,df->isf/dot_general | solution.py:226
  359.9 13.3 %all-gather.1 = bf16[4,729,16]{1,2,0:T(8,128)(2,1)S(1)} all-gather(bf16[1,729,16]{1,2,0:T(8,128)(2,1)S(1)} %fusion.92), channel_id=2, replica_groups=mesh['fsdp'=4,'heads'=2,'tensor'=4] {'tensor'}, dimensions={0}, use_global_device_ids=true | all-gather | bytes 116640 | tf_op jit(solution)/shard_map/all_gather | solution.py:189
  373.2 13.1 %all-gather.19.cloned.1.call-done = bf16[1152,1076]{1,0:T(8,128)(2,1)} async-done(((bf16[288,1076]{1,0:T(8,128)(2,1)}), bf16[1152,1076]{1,0:T(8,128)(2,1)}) %all-gather.19.cloned.1.call-update) | async-done | bytes 2479120 | tf_op jit(solution)/shard_map/all_gather | solution.py:122
  386.4 124.8 %all-gather.17.cloned.1.call-done = bf16[4,729,1152]{2,1,0:T(8,128)(2,1)} async-done(((bf16[1,729,1152]{2,1,0:T(8,128)(2,1)}), bf16[4,729,1152]{2,1,0:T(8,128)(2,1)}) %all-gather.17.cloned.1.call-update) | async-done | bytes 6718480 | tf_op jit(solution)/shard_map/all_gather | solution.py:188
  511.2 12.4 fusion.75
  523.6 10.1 multiply_convert_fusion.1
  533.7 18.5 %fusion.50 = bf16[4,729,1076]{1,2,0:T(8,128)(2,1)S(1)} fusion(f32[4,729,1076]{1,2,0:T(8,128)} %get-tuple-element.204, f32[4,729,1076]{1,2,0:T(8,128)} %fusion.69, f32[4,16,729]{2,1,0:T(8,128)S(1)} %fusion.138, bf16[4,16,1076]{2,1,0:T(8,128)(2,1)S(1)} %gather_fusion.7), kind=kOutput, calls=%fused_computation.72 | convolution fusion | flops 668312192 | bytes 31700512 | tf_op jit(solution)/shard_map/cbd,cdp->cbp/dot_general | solution.py:227
  555.9 13.1 %fusion.73 = f32[4,729,1152]{2,1,0:T(8,128)} fusion(bf16[4,729,1076]{1,2,0:T(8,128)(2,1)S(1)} %fusion.50, bf16[1152,1076]{1,0:T(8,128)(2,1)S(1)} %copy-done.56), kind=kOutput, calls=%fused_computation.118 | convolution fusion | flops 7229067264 | bytes 22191264 | tf_op jit(solution)/shard_map/isf,df->isd/dot_general | solution.py:235
  569.0 10.8 add_convert_fusion
  583.9 13.5 %fusion.71 = f32[4,729,1152]{2,1,0:T(8,128)S(1)} fusion(bf16[4,729,1076]{1,2,0:T(8,128)(2,1)} %get-tuple-element.203, bf16[1152,1076]{1,0:T(8,128)(2,1)S(1)} %copy-done.55), kind=kOutput, calls=%fused_computation.116 | convolution fusion | flops 7229067264 | bytes 22191264 | tf_op jit(solution)/shard_map/isf,df->isd/dot_general | solution.py:210
  606.6 90.2 %reduce-scatter.9.cloned.1.call-done = bf16[1,729,1152]{2,1,0:T(8,128)(2,1)} async-done(((bf16[4,729,1152]{2,1,0:T(8,128)(2,1)}), bf16[1,729,1152]{2,1,0:T(8,128)(2,1)}) %reduce-scatter.9.cloned.1.call-update) | async-done | bytes 1679632 | tf_op jit(solution)/shard_map/reduce_scatter | solution.py:242
  700.4 118.0 %reduce-scatter.7.cloned.1.call-done = bf16[1,729,1152]{2,1,0:T(8,128)(2,1)} async-done(((bf16[4,729,1152]{2,1,0:T(8,128)(2,1)}), bf16[1,729,1152]{2,1,0:T(8,128)(2,1)}) %reduce-scatter.7.cloned.1.call-update) | async-done | bytes 1679632 | tf_op jit(solution)/shard_map/reduce_scatter | solution.py:217
  863.4 99.9 %while.29 = (s32[]{:T(128)}, bf16[2,729,8,72]{1,3,2,0:T(8,128)(2,1)}, bf16[2,729,8,72]{1,3,2,0:T(8,128)(2,1)}, bf16[2,729,8,72]{1,3,2,0:T(8,128)(2,1)}, bf16[2,7...) while((s32[]{:T(128)}, ...), condition=%wide.region_15.16_spmd, body=%wide.region_13.15_spmd.sunk | while | flops 3112952320 | bytes 200497152 | solution.py:272
  863.9 10.1 fusion.216
  882.1 12.7 %multiply_reduce_fusion.9 = (f32[8,729]{1,0:T(8,128)S(1)}, f32[8,729,729]{1,2,0:T(8,128)}) fusion(f32[8,729,729]{1,2,0:T(8,128)} %fusion.216, f32[8,729]{1,0:T(8,128)S(1)} %dynamic-slice_bitcast_fusion.2, bf16[2,729,8,72]{1,3,2,0:T(8,128)(2,1)S(1)} %copy-done.13, s32[]{:T(128)S(6)} %copy.187, bf16[2,729,8,72]{1,3,2,0:T(8,128)(2,1)S(1)} %copy-done.9), kind=kOutput, calls=%fused_computation.30.clone.1 | convolution fusion | flops 629220288 | bytes 35830624 | tf_op jit(solution)/shard_map/while/body/eval_jaxpr/qhd,khd->hqk/dot_general | solution.py:58
  894.8 13.2 %multiply_convert_fusion.3 = bf16[8,729,729]{1,2,0:T(8,128)(2,1)S(1)} fusion(f32[8,729,729]{1,2,0:T(8,128)} %get-tuple-element.305, f32[8,729,729]{1,2,0:T(8,128)} %fusion.216, f32[8,729]{1,0:T(8,128)S(1)} %get-tuple-element.306, f32[8,729]{1,0:T(8,128)S(1)} %dynamic-slice_bitcast_fusion.2), kind=kLoop, calls=%fused_computation.29.clone.1 | loop fusion | flops 21257640 | bytes 42561936 | tf_op jit(solution)/shard_map/while/body/eval_jaxpr/convert_element_type | solution.py:63
  913.8 10.0 fusion.216
  932.0 12.6 multiply_reduce_fusion.9
  944.5 13.1 %multiply_convert_fusion.3 = bf16[8,729,729]{1,2,0:T(8,128)(2,1)S(1)} fusion(f32[8,729,729]{1,2,0:T(8,128)} %get-tuple-element.305, f32[8,729,729]{1,2,0:T(8,128)} %fusion.216, f32[8,729]{1,0:T(8,128)S(1)} %get-tuple-element.306, f32[8,729]{1,0:T(8,128)S(1)} %dynamic-slice_bitcast_fusion.2), kind=kLoop, calls=%fused_computation.29.clone.1 | loop fusion | flops 21257640 | bytes 42561936 | tf_op jit(solution)/shard_map/while/body/eval_jaxpr/convert_element_type | solution.py:63
  983.7 11.9 fusion.57
  1011.3 76.5 %all-reduce.9.cloned.1.call-done = (f32[3,8,16,576]{3,1,2,0:T(8,128)}, f32[8,576,16]{1,0,2:T(8,128)}) async-done(((f32[3,8,16,576]{3,1,2,0:T(8,128)}, f32[8,576,16]{1,0,2:T(8,128)}), (f32[3,8,16,576]{3,1,2,0:T(8,128)}, f32[8,576,16]{1,0,2:T(8,128)})) %all-reduce.9.cloned.1.call-update) | async-done | bytes 1179664 | tf_op jit(solution)/shard_map/psum | solution.py:321
  1091.8 142.8 %all-reduce.7.cloned.1.call-done = (f32[3,8,1152,16]{2,1,3,0:T(8,128)}, f32[8,16,1152]{2,0,1:T(8,128)}, f32[8,1152,16]{1,0,2:T(8,128)}, f32[8,16,1152]{2,0,1:T(8,128)}) async-done(((f32[3,8,1152,16]{2,1,3,0:T(8,128)}, f32[8,16,1152]{2,0,1:T(8,128)}, f32[8,1152,16]{1,0,2:T(8,128)}, f32[8,16,1152]{2,0,1:T(8,128)}), (f32[3,8,1152,16]{2,1,3,0:T(8,128)}, f32[8,16,1152]{2,0,1:T(8,128)}, f32[8,1152,16]{1,0,2:T(8,128)}, ...) | async-done | bytes 3538960 | tf_op jit(solution)/shard_map/psum | solution.py:317
  (288 shorter events, 242.4 us)
Async XLA Ops:
  8.0 17.2 %copy-start = (bf16[3,8,1152,16]{2,3,1,0:T(8,128)(2,1)S(1)}, bf16[3,8,1152,16]{2,3,1,0:T(8,128)(2,1)}, u32[]{:S(2)}) copy-start(bf16[3,8,1152,16]{2,3,1,0:T(8,128)(2,1)} %param.38) | copy-start | bytes 2654212
  8.0 25.2 %all-gather.11.cloned.1.call-start = ((), (), s32[]{:S(2)}) async-start(), calls=%async_computation.4 | async-start | bytes 5087232 | tf_op jit(solution)/shard_map/all_gather | solution.py:126
  17.9 73.0 %all-gather.13.cloned.1.call-start = ((), (), s32[]{:S(2)}) async-start(), calls=%async_computation.5 | async-start | bytes 5529600 | tf_op jit(solution)/shard_map/all_gather | solution.py:120
  18.6 150.3 %all-gather.15.cloned.1.call-start = ((), (), s32[]{:S(2)}) async-start(), calls=%async_computation.6 | async-start | bytes 1843200 | tf_op jit(solution)/shard_map/all_gather | solution.py:121
  19.4 170.4 %reduce-scatter.5.cloned.1.call-start = ((), (), s32[]{:S(2)}) async-start(), calls=%async_computation.7 | async-start | bytes 5087232 | tf_op jit(solution)/shard_map/reduce_scatter | solution.py:176
  25.2 76.4 %copy-start.32 = (bf16[2,3,16,576]{3,2,1,0:T(8,128)(2,1)}, bf16[2,3,16,576]{3,2,1,0:T(8,128)(2,1)S(1)}, u32[]{:S(2)}) copy-start(bf16[2,3,16,576]{3,2,1,0:T(8,128)(2,1)S(1)} %gather_fusion.2) | copy-start | bytes 331780
  25.8 75.8 %copy-start.11 = (bf16[2,3,1152,16]{2,3,1,0:T(8,128)(2,1)}, bf16[2,3,1152,16]{2,3,1,0:T(8,128)(2,1)S(1)}, u32[]{:S(2)}) copy-start(bf16[2,3,1152,16]{2,3,1,0:T(8,128)(2,1)S(1)} %gather_fusion.1) | copy-start | bytes 663556
  36.3 65.4 %copy-start.25 = (f32[3,2,729,16]{2,3,0,1:T(8,128)}, f32[3,2,729,16]{2,3,0,1:T(8,128)S(1)}, u32[]{:S(2)}) copy-start(f32[3,2,729,16]{2,3,0,1:T(8,128)S(1)} %fusion.86) | copy-start | bytes 839812
  109.1 57.2 %copy-start.21 = (bf16[2,576,16]{1,2,0:T(8,128)(2,1)S(1)}, bf16[2,576,16]{1,2,0:T(8,128)(2,1)}, u32[]{:S(2)}) copy-start(bf16[2,576,16]{1,2,0:T(8,128)(2,1)} %gather_fusion.3) | copy-start | bytes 110596
  178.4 126.8 %all-gather.23.cloned.1.call-start = ((), (), s32[]{:S(2)}) async-start(), calls=%async_computation.12 | async-start | bytes 8478720 | tf_op jit(solution)/shard_map/all_gather | solution.py:222
  181.8 163.1 %all-gather.21.cloned.1.call-start = ((), (), s32[]{:S(2)}) async-start(), calls=%async_computation.10 | async-start | bytes 3317760 | tf_op jit(solution)/shard_map/all_gather | solution.py:123
  182.4 204.0 %all-gather.19.cloned.1.call-start = ((), (), s32[]{:S(2)}) async-start(), calls=%async_computation.9 | async-start | bytes 3317760 | tf_op jit(solution)/shard_map/all_gather | solution.py:122
  182.9 328.3 %all-gather.17.cloned.1.call-start = ((), (), s32[]{:S(2)}) async-start(), calls=%async_computation.8 | async-start | bytes 8478720 | tf_op jit(solution)/shard_map/all_gather | solution.py:188
  196.7 500.0 %reduce-scatter.9.cloned.1.call-start = ((), (), s32[]{:S(2)}) async-start(), calls=%async_computation.13 | async-start | bytes 8478720 | tf_op jit(solution)/shard_map/reduce_scatter | solution.py:242
  310.0 49.4 %copy-start.14 = (bf16[1,729,1152]{2,1,0:T(8,128)(2,1)S(1)}, bf16[1,729,1152]{2,1,0:T(8,128)(2,1)}, u32[]{:S(2)}) copy-start(bf16[1,729,1152]{2,1,0:T(8,128)(2,1)} %add_convert_fusion.4) | copy-start | bytes 5038852
  373.2 150.3 %copy-start.34 = (bf16[4,729,16]{1,2,0:T(8,128)(2,1)}, bf16[4,729,16]{1,2,0:T(8,128)(2,1)S(1)}, u32[]{:S(2)}) copy-start(bf16[4,729,16]{1,2,0:T(8,128)(2,1)S(1)} %all-gather.1) | copy-start | bytes 279940
  579.8 238.6 %reduce-scatter.7.cloned.1.call-start = ((), (), s32[]{:S(2)}) async-start(), calls=%async_computation.11 | async-start | bytes 8478720 | tf_op jit(solution)/shard_map/reduce_scatter | solution.py:217
  605.9 245.4 %all-gather.25.cloned.1.call-start = ((), (), s32[]{:S(2)}) async-start(), calls=%async_computation.14 | async-start | bytes 5087232 | tf_op jit(solution)/shard_map/all_gather | solution.py:261
  696.8 121.6 %copy-start.18 = (bf16[1,729,1152]{2,1,0:T(8,128)(2,1)S(1)}, bf16[1,729,1152]{2,1,0:T(8,128)(2,1)}, u32[]{:S(2)}) copy-start(bf16[1,729,1152]{2,1,0:T(8,128)(2,1)} %reduce-scatter.9.cloned.1.call-done) | copy-start | bytes 5038852
  824.8 175.7 %all-reduce.11.cloned.1.call-start = ((), (), s32[]{:S(2)}) async-start(), calls=%async_computation.18 | async-start | bytes 1179648 | tf_op jit(solution)/shard_map/psum | solution.py:325
  833.7 13.3 %slice-start = ((s8[6782976]{0:T(1024)(128)(4,1)}), s8[2588672]{0:T(1024)(128)(4,1)S(1)}, s32[]{:S(2)}) async-start(s8[6782976]{0:T(1024)(128)(4,1)} %bitcast.261), calls=%async_computation.19 | async-start | bytes 5177344
  851.2 236.6 %all-reduce.9.cloned.1.call-start = ((), (), s32[]{:S(2)}) async-start(), calls=%async_computation.17 | async-start | bytes 2621440 | tf_op jit(solution)/shard_map/psum | solution.py:321
  863.4 99.9 %copy-start.26 = (f32[3,2,729,16]{2,3,0,1:T(8,128)S(1)}, f32[3,2,729,16]{2,3,0,1:T(8,128)}, u32[]{:S(2)}) copy-start(f32[3,2,729,16]{2,3,0,1:T(8,128)} %copy-done.25) | copy-start | bytes 839812
  894.8 13.3 %copy-start.6 = (bf16[2,729,8,72]{1,3,2,0:T(8,128)(2,1)S(1)}, bf16[2,729,8,72]{1,3,2,0:T(8,128)(2,1)}, u32[]{:S(2)}) copy-start(bf16[2,729,8,72]{1,3,2,0:T(8,128)(2,1)} %get-tuple-element.353) | copy-start | bytes 5038852 | tf_op jit(solution)/shard_map/while
  894.8 13.3 %copy-start.60 = (bf16[2,729,8,72]{1,3,2,0:T(8,128)(2,1)S(1)}, bf16[2,729,8,72]{1,3,2,0:T(8,128)(2,1)}, u32[]{:S(2)}) copy-start(bf16[2,729,8,72]{1,3,2,0:T(8,128)(2,1)} %get-tuple-element.340) | copy-start | bytes 5038852 | tf_op jit(solution)/shard_map/while
  944.5 13.1 %copy-start.6 = (bf16[2,729,8,72]{1,3,2,0:T(8,128)(2,1)S(1)}, bf16[2,729,8,72]{1,3,2,0:T(8,128)(2,1)}, u32[]{:S(2)}) copy-start(bf16[2,729,8,72]{1,3,2,0:T(8,128)(2,1)} %get-tuple-element.353) | copy-start | bytes 5038852 | tf_op jit(solution)/shard_map/while
  944.5 13.1 %copy-start.60 = (bf16[2,729,8,72]{1,3,2,0:T(8,128)(2,1)S(1)}, bf16[2,729,8,72]{1,3,2,0:T(8,128)(2,1)}, u32[]{:S(2)}) copy-start(bf16[2,729,8,72]{1,3,2,0:T(8,128)(2,1)} %get-tuple-element.340) | copy-start | bytes 5038852 | tf_op jit(solution)/shard_map/while
  972.4 262.2 %all-reduce.7.cloned.1.call-start = ((), (), s32[]{:S(2)}) async-start(), calls=%async_computation.16 | async-start | bytes 7077888 | tf_op jit(solution)/shard_map/psum | solution.py:317
  983.7 263.7 %reduce-scatter.11.cloned.1.call-start = ((), (), s32[]{:S(2)}) async-start(), calls=%async_computation.15 | async-start | bytes 5087232 | tf_op jit(solution)/shard_map/reduce_scatter | solution.py:292
  1234.6 12.7 %copy-start.40 = (f32[729]{0:T(1024)S(1)}, f32[729]{0:T(1024)}, u32[]{:S(2)}) copy-start(f32[729]{0:T(1024)} %copy-done.39) | copy-start | bytes 8752
  1234.6 12.7 %copy-start.43 = (f32[1152]{0:T(1024)S(1)}, f32[1152]{0:T(1024)}, u32[]{:S(2)}) copy-start(f32[1152]{0:T(1024)} %param.28) | copy-start | bytes 13828
  1234.7 12.7 %copy-start.48 = (f32[729]{0:T(1024)S(1)}, f32[729]{0:T(1024)}, u32[]{:S(2)}) copy-start(f32[729]{0:T(1024)} %copy-done.47) | copy-start | bytes 8752
  (60 other events, 316.2 us)
Sparse Core Ops, SparseCore 0:
  18.0 15.1 all-gather.10
  35.0 55.7 all-gather.12
  92.7 30.1 all-gather.14
  178.5 11.2 reduce-scatter.4
  824.9 12.9 all-gather.24
  851.3 55.7 all-reduce.10
  972.6 115.1 all-reduce.8
  1094.9 139.7 all-reduce.6
  1237.0 10.2 reduce-scatter.10
Sparse Core Ops, SparseCore 1:
  181.9 123.2 all-gather.22
  306.9 37.9 all-gather.20
  346.6 39.7 all-gather.18
  387.9 123.2 all-gather.16
  579.9 116.8 reduce-scatter.8
  699.2 119.1 reduce-scatter.6
where the time goes:
time: 1270 us
  waiting for transfers between devices  781 us (61%)
  matrix products  326 us (26%)
  other arithmetic  77 us (6%)
  local copies, waits for them, and re-layouts  49.9 us (4%)
  between operations  18.4 us (1%)
  blocking collectives  13.3 us (1%)
    psum x1, waiting for transfers between devices, per_device(): lax.psum((grad_qkv_in_part, grad_proj_out_part, grad_up_in_part, grad_dow...  143 us
    all_gather x1, waiting for transfers between devices, per_device(): lax.all_gather(second_norm_reduced, 'tensor', axis=0, tiled=True)  125 us
    reduce_scatter x1, waiting for transfers between devices, per_device(): lax.psum_scatter(mlp_part.astype(jnp.bfloat16), 'tensor', scatter_dimensi...  118 us
    all_gather x1, waiting for transfers between devices, per_device(): grad_mlp_in = lax.all_gather(grad_mlp, 'tensor', axis=0, tiled=True)  103 us
    reduce_scatter x1, waiting for transfers between devices, per_device(): lax.psum_scatter(grad_ln2.astype(jnp.bfloat16), 'tensor', scatter_dimensi...  90.2 us
    psum x1, waiting for transfers between devices, per_device(): lax.psum((grad_qkv_out_part, grad_proj_in_part), ('fsdp', 'tensor'))  76.5 us
    all_gather x1, waiting for transfers between devices, per_device(): lax.all_gather(query_key_value_weight, 'fsdp', axis=0, tiled=True)  54.6 us
    unnamed x129, local copies, waits for them, and re-layouts  35.5 us
  transfers between devices with their start and end apart: 15, of which 12 were waited for; matrix products, arithmetic and copies ran while one was open for 27% of the time, Pallas kernels for 0%

commit v1 on v0

--- a/solution.py
+++ b/solution.py
@@ -315,8 +315,11 @@
         ),
     )
     grad_qkv_in, grad_proj_out, grad_up_in, grad_down_out = lax.psum(
-        (grad_qkv_in_part, grad_proj_out_part, grad_up_in_part, grad_down_out_part),
-        ("fsdp", "heads", "tensor"),
+        lax.psum(
+            (grad_qkv_in_part, grad_proj_out_part, grad_up_in_part, grad_down_out_part),
+            axis_name=("heads", "tensor"),
+        ),
+        axis_name="fsdp",
     )
     grad_qkv_out, grad_proj_in = lax.psum(
         (grad_qkv_out_part, grad_proj_in_part), ("fsdp", "tensor")

time: 1270 us -> 1360 us (1.071)
  waiting for transfers between devices: 781 us -> 866 us
    psum x0 -> x1, waiting for transfers between devices: none -> 93.4 us  [per_device(): lax.psum(lax.psum((grad_qkv_in_part, grad_proj_out_part, grad_up_in_part,...]
    psum x1, waiting for transfers between devices: 143 us -> 60.8 us  [per_device(): lax.psum((grad_qkv_in_part, grad_proj_out_part, grad_up_in_part, grad_dow...]
    psum x1, waiting for transfers between devices: 0.02 us -> 42.1 us  [per_device(): lax.psum(grad_up_out_part.astype(jnp.bfloat16), ('fsdp', 'heads'))]
    psum x1, waiting for transfers between devices: 76.5 us -> 109 us  [per_device(): lax.psum((grad_qkv_out_part, grad_proj_in_part), ('fsdp', 'tensor'))]
    unnamed x129 -> x121, local copies, waits for them, and re-layouts: 35.5 us -> 34.7 us
  transfers between devices with their start and end apart: 15 -> 16, of which waited for: 12 -> 14; matrix products, arithmetic and copies ran while one was open for 27% -> 17% of each run, Pallas kernels for 0% -> 0%
where the time goes in v1:
time: 1360 us
  waiting for transfers between devices  866 us (64%)
  matrix products  329 us (24%)
  other arithmetic  77.4 us (6%)
  local copies, waits for them, and re-layouts  49.9 us (4%)
  between operations  18.7 us (1%)
    all_gather x1, waiting for transfers between devices, per_device(): lax.all_gather(second_norm_reduced, 'tensor', axis=0, tiled=True)  125 us
    reduce_scatter x1, waiting for transfers between devices, per_device(): lax.psum_scatter(mlp_part.astype(jnp.bfloat16), 'tensor', scatter_dimensi...  118 us
    psum x1, waiting for transfers between devices, per_device(): lax.psum((grad_qkv_out_part, grad_proj_in_part), ('fsdp', 'tensor'))  109 us
    all_gather x1, waiting for transfers between devices, per_device(): grad_mlp_in = lax.all_gather(grad_mlp, 'tensor', axis=0, tiled=True)  102 us
    psum x1, waiting for transfers between devices, per_device(): lax.psum(lax.psum((grad_qkv_in_part, grad_proj_out_part, grad_up_in_part,...  93.4 us
    reduce_scatter x1, waiting for transfers between devices, per_device(): lax.psum_scatter(grad_ln2.astype(jnp.bfloat16), 'tensor', scatter_dimensi...  90.3 us
    psum x1, waiting for transfers between devices, per_device(): lax.psum((grad_qkv_in_part, grad_proj_out_part, grad_up_in_part, grad_dow...  60.8 us
    all_gather x1, waiting for transfers between devices, per_device(): lax.all_gather(query_key_value_weight, 'fsdp', axis=0, tiled=True)  54.6 us
  transfers between devices with their start and end apart: 16, of which 14 were waited for; matrix products, arithmetic and copies ran while one was open for 17% of the time, Pallas kernels for 0%

profile of v1, /device:TPU:0, one launch (start us, length us, event | category | flops | bytes accessed | tf_op | source)
XLA Modules:
  0.0 1356.4 jit_solution(8893954172976958505)
XLA Ops:
  36.3 54.6 %all-gather.13.cloned.1.call-done = bf16[1152,3,576]{2,0,1:T(8,128)(2,1)} async-done(((bf16[288,3,576]{2,0,1:T(8,128)(2,1)}), bf16[1152,3,576]{2,0,1:T(8,128)(2,1)}) %all-gather.13.cloned.1.call-update) | async-done | bytes 3981328 | tf_op jit(solution)/shard_map/all_gather | solution.py:120
  90.9 10.7 fusion.59
  109.1 57.1 %while.28 = (s32[]{:T(128)}, bf16[2,729,8,72]{1,3,2,0:T(8,128)(2,1)}, f32[2,8,729]{2,1,0:T(8,128)S(1)}, bf16[2,729,8,72]{1,3,2,0:T(8,128)(2,1)}, bf16[2,729,8,72...) while((s32[]{:T(128)}, bf16[2,729,8,72]{1,3,2,0:T(8,128)(2,1)}, ...), condition=%wide.region_5.6_spmd, body=%wide.region_2.5_spmd.sunk | while | flops 1263117824 | bytes 55831608 | solution.py:160
  109.1 10.0 multiply_reduce_fusion.8
  128.2 9.3 fusion.207
  137.5 9.9 multiply_reduce_fusion.8
  202.6 101.7 %all-gather.23.cloned.1.call-done = bf16[4,729,1152]{2,1,0:T(8,128)(2,1)} async-done(((bf16[1,729,1152]{2,1,0:T(8,128)(2,1)}), bf16[4,729,1152]{2,1,0:T(8,128)(2,1)}) %all-gather.23.cloned.1.call-update) | async-done | bytes 6718480 | tf_op jit(solution)/shard_map/all_gather | solution.py:222
  309.2 34.9 %all-gather.21.cloned.1.call-done = bf16[1152,1076]{1,0:T(8,128)(2,1)} async-done(((bf16[288,1076]{1,0:T(8,128)(2,1)}), bf16[1152,1076]{1,0:T(8,128)(2,1)}) %all-gather.21.cloned.1.call-update) | async-done | bytes 2479120 | tf_op jit(solution)/shard_map/all_gather | solution.py:123
  344.0 14.7 %fusion.69 = f32[4,729,1076]{1,2,0:T(8,128)} fusion(bf16[4,729,1152]{2,1,0:T(8,128)(2,1)} %all-gather.23.cloned.1.call-done, bf16[1152,1076]{1,0:T(8,128)(2,1)} %all-gather.21.cloned.1.call-done), kind=kOutput, calls=%fused_computation.114 | convolution fusion | flops 7229067264 | bytes 21748032 | tf_op jit(solution)/shard_map/isd,df->isf/dot_general | solution.py:226
  359.3 13.4 all-gather.1
  372.7 12.8 all-gather.19.cloned.1.call-done
  385.5 124.8 %all-gather.17.cloned.1.call-done = bf16[4,729,1152]{2,1,0:T(8,128)(2,1)} async-done(((bf16[1,729,1152]{2,1,0:T(8,128)(2,1)}), bf16[4,729,1152]{2,1,0:T(8,128)(2,1)}) %all-gather.17.cloned.1.call-update) | async-done | bytes 6718480 | tf_op jit(solution)/shard_map/all_gather | solution.py:188
  510.4 12.6 fusion.75
  523.0 10.1 multiply_convert_fusion.1
  533.1 18.4 %fusion.50 = bf16[4,729,1076]{1,2,0:T(8,128)(2,1)S(1)} fusion(f32[4,729,1076]{1,2,0:T(8,128)} %get-tuple-element.208, f32[4,729,1076]{1,2,0:T(8,128)} %fusion.69, f32[4,16,729]{2,1,0:T(8,128)S(1)} %fusion.138, bf16[4,16,1076]{2,1,0:T(8,128)(2,1)S(1)} %gather_fusion.7), kind=kOutput, calls=%fused_computation.72 | convolution fusion | flops 668312192 | bytes 31700512 | tf_op jit(solution)/shard_map/cbd,cdp->cbp/dot_general | solution.py:227
  555.3 13.3 fusion.73
  568.5 10.8 add_convert_fusion
  583.4 13.4 fusion.71
  606.0 90.3 %reduce-scatter.9.cloned.1.call-done = bf16[1,729,1152]{2,1,0:T(8,128)(2,1)} async-done(((bf16[4,729,1152]{2,1,0:T(8,128)(2,1)}), bf16[1,729,1152]{2,1,0:T(8,128)(2,1)}) %reduce-scatter.9.cloned.1.call-update) | async-done | bytes 1679632 | tf_op jit(solution)/shard_map/reduce_scatter | solution.py:242
  699.8 118.1 %reduce-scatter.7.cloned.1.call-done = bf16[1,729,1152]{2,1,0:T(8,128)(2,1)} async-done(((bf16[4,729,1152]{2,1,0:T(8,128)(2,1)}), bf16[1,729,1152]{2,1,0:T(8,128)(2,1)}) %reduce-scatter.7.cloned.1.call-update) | async-done | bytes 1679632 | tf_op jit(solution)/shard_map/reduce_scatter | solution.py:217
  848.2 99.5 %while.29 = (s32[]{:T(128)}, bf16[2,729,8,72]{1,3,2,0:T(8,128)(2,1)}, bf16[2,729,8,72]{1,3,2,0:T(8,128)(2,1)}, bf16[2,729,8,72]{1,3,2,0:T(8,128)(2,1)}, bf16[2,7...) while((s32[]{:T(128)}, ...), condition=%wide.region_15.16_spmd, body=%wide.region_13.15_spmd.sunk | while | flops 3112952320 | bytes 200497152 | solution.py:272
  848.4 10.1 fusion.216
  866.6 12.5 multiply_reduce_fusion.9
  879.1 13.2 multiply_convert_fusion.3
  898.1 10.1 fusion.216
  916.3 12.5 multiply_reduce_fusion.9
  928.8 13.2 multiply_convert_fusion.3
  985.4 60.8 %all-reduce.11.cloned.1.call-done = (f32[3,8,1152,16]{2,1,3,0:T(8,128)}, f32[8,16,1152]{2,0,1:T(8,128)}, f32[8,1152,16]{1,0,2:T(8,128)}, f32[8,16,1152]{2,0,1:T(8,128)}) async-done(((f32[3,8,1152,16]{2,1,3,0:T(8,128)}, f32[8,16,1152]{2,0,1:T(8,128)}, f32[8,1152,16]{1,0,2:T(8,128)}, f32[8,16,1152]{2,0,1:T(8,128)}), (f32[3,8,1152,16]{2,1,3,0:T(8,128)}, f32[8,16,1152]{2,0,1:T(8,128)}, ...) | async-done | bytes 3538960 | tf_op jit(solution)/shard_map/psum | solution.py:318
  1046.7 11.8 fusion.57
  1063.3 42.1 %all-reduce.15.cloned.1.call-done = (bf16[8,16,1076]{2,0,1:T(8,128)(2,1)}, bf16[8,16,1076]{2,0,1:T(8,128)(2,1)}) async-done(((bf16[8,16,1076]{2,0,1:T(8,128)(2,1)}, bf16[8,16,1076]{2,0,1:T(8,128)(2,1)}), (bf16[8,16,1076]{2,0,1:T(8,128)(2,1)}, bf16[8,16,1076]{2,0,1:T(8,128)(2,1)})) %all-reduce.15.cloned.1.call-update) | async-done | bytes 550928 | tf_op jit(solution)/shard_map/psum | solution.py:328
  1116.2 108.9 %all-reduce.9.cloned.1.call-done = (f32[3,8,16,576]{3,1,2,0:T(8,128)}, f32[8,576,16]{1,0,2:T(8,128)}) async-done(((f32[3,8,16,576]{3,1,2,0:T(8,128)}, f32[8,576,16]{1,0,2:T(8,128)}), (f32[3,8,16,576]{3,1,2,0:T(8,128)}, f32[8,576,16]{1,0,2:T(8,128)})) %all-reduce.9.cloned.1.call-update) | async-done | bytes 1179664 | tf_op jit(solution)/shard_map/psum | solution.py:324
  1229.2 93.4 %all-reduce.13.cloned.1.call-done = (f32[3,8,1152,16]{2,1,3,0:T(8,128)}, f32[8,16,1152]{2,0,1:T(8,128)}, f32[8,1152,16]{1,0,2:T(8,128)}, f32[8,16,1152]{2,0,1:T(8,128)}) async-done(((f32[3,8,1152,16]{2,1,3,0:T(8,128)}, f32[8,16,1152]{2,0,1:T(8,128)}, f32[8,1152,16]{1,0,2:T(8,128)}, f32[8,16,1152]{2,0,1:T(8,128)}), (f32[3,8,1152,16]{2,1,3,0:T(8,128)}, f32[8,16,1152]{2,0,1:T(8,128)}, ...) | async-done | bytes 3538960 | tf_op jit(solution)/shard_map/psum | solution.py:317
  (282 shorter events, 264.8 us)
Async XLA Ops:
  8.0 17.6 %copy-start = (bf16[3,8,1152,16]{2,3,1,0:T(8,128)(2,1)S(1)}, bf16[3,8,1152,16]{2,3,1,0:T(8,128)(2,1)}, u32[]{:S(2)}) copy-start(bf16[3,8,1152,16]{2,3,1,0:T(8,128)(2,1)} %param.38) | copy-start | bytes 2654212
  8.0 25.2 %all-gather.11.cloned.1.call-start = ((), (), s32[]{:S(2)}) async-start(), calls=%async_computation.4 | async-start | bytes 5087232 | tf_op jit(solution)/shard_map/all_gather | solution.py:126
  17.9 73.0 %all-gather.13.cloned.1.call-start = ((), (), s32[]{:S(2)}) async-start(), calls=%async_computation.5 | async-start | bytes 5529600 | tf_op jit(solution)/shard_map/all_gather | solution.py:120
  18.6 149.4 %all-gather.15.cloned.1.call-start = ((), (), s32[]{:S(2)}) async-start(), calls=%async_computation.6 | async-start | bytes 1843200 | tf_op jit(solution)/shard_map/all_gather | solution.py:121
  19.4 169.6 %reduce-scatter.5.cloned.1.call-start = ((), (), s32[]{:S(2)}) async-start(), calls=%async_computation.7 | async-start | bytes 5087232 | tf_op jit(solution)/shard_map/reduce_scatter | solution.py:176
  25.6 76.0 %copy-start.32 = (bf16[2,3,16,576]{3,2,1,0:T(8,128)(2,1)}, bf16[2,3,16,576]{3,2,1,0:T(8,128)(2,1)S(1)}, u32[]{:S(2)}) copy-start(bf16[2,3,16,576]{3,2,1,0:T(8,128)(2,1)S(1)} %gather_fusion.2) | copy-start | bytes 331780
  26.2 75.4 %copy-start.9 = (bf16[2,3,1152,16]{2,3,1,0:T(8,128)(2,1)}, bf16[2,3,1152,16]{2,3,1,0:T(8,128)(2,1)S(1)}, u32[]{:S(2)}) copy-start(bf16[2,3,1152,16]{2,3,1,0:T(8,128)(2,1)S(1)} %gather_fusion.1) | copy-start | bytes 663556
  36.3 65.4 %copy-start.21 = (f32[3,2,729,16]{2,3,0,1:T(8,128)}, f32[3,2,729,16]{2,3,0,1:T(8,128)S(1)}, u32[]{:S(2)}) copy-start(f32[3,2,729,16]{2,3,0,1:T(8,128)S(1)} %fusion.86) | copy-start | bytes 839812
  109.1 57.1 %copy-start.18 = (bf16[2,576,16]{1,2,0:T(8,128)(2,1)S(1)}, bf16[2,576,16]{1,2,0:T(8,128)(2,1)}, u32[]{:S(2)}) copy-start(bf16[2,576,16]{1,2,0:T(8,128)(2,1)} %gather_fusion.3) | copy-start | bytes 110596
  177.5 126.8 %all-gather.23.cloned.1.call-start = ((), (), s32[]{:S(2)}) async-start(), calls=%async_computation.12 | async-start | bytes 8478720 | tf_op jit(solution)/shard_map/all_gather | solution.py:222
  181.0 163.1 %all-gather.21.cloned.1.call-start = ((), (), s32[]{:S(2)}) async-start(), calls=%async_computation.10 | async-start | bytes 3317760 | tf_op jit(solution)/shard_map/all_gather | solution.py:123
  181.6 203.9 %all-gather.19.cloned.1.call-start = ((), (), s32[]{:S(2)}) async-start(), calls=%async_computation.9 | async-start | bytes 3317760 | tf_op jit(solution)/shard_map/all_gather | solution.py:122
  182.1 328.2 %all-gather.17.cloned.1.call-start = ((), (), s32[]{:S(2)}) async-start(), calls=%async_computation.8 | async-start | bytes 8478720 | tf_op jit(solution)/shard_map/all_gather | solution.py:188
  196.0 500.3 %reduce-scatter.9.cloned.1.call-start = ((), (), s32[]{:S(2)}) async-start(), calls=%async_computation.13 | async-start | bytes 8478720 | tf_op jit(solution)/shard_map/reduce_scatter | solution.py:242
  198.6 638.3 %copy-start.47 = (s32[4]{0:T(128)}, s32[4]{0:T(128)S(1)}, u32[]{:S(2)}) copy-start(s32[4]{0:T(128)S(1)} %gather_fusion.5) | copy-start | bytes 52
  309.2 223.9 %copy-start.25 = (f32[4,16,729]{2,1,0:T(8,128)}, f32[4,16,729]{2,1,0:T(8,128)S(1)}, u32[]{:S(2)}) copy-start(f32[4,16,729]{2,1,0:T(8,128)S(1)} %fusion.138) | copy-start | bytes 559876
  344.0 14.7 %copy-start.12 = (bf16[1,729,1152]{2,1,0:T(8,128)(2,1)S(1)}, bf16[1,729,1152]{2,1,0:T(8,128)(2,1)}, u32[]{:S(2)}) copy-start(bf16[1,729,1152]{2,1,0:T(8,128)(2,1)} %add_convert_fusion.4) | copy-start | bytes 5038852
  372.7 150.3 %copy-start.34 = (bf16[4,729,16]{1,2,0:T(8,128)(2,1)}, bf16[4,729,16]{1,2,0:T(8,128)(2,1)S(1)}, u32[]{:S(2)}) copy-start(bf16[4,729,16]{1,2,0:T(8,128)(2,1)S(1)} %all-gather.1) | copy-start | bytes 279940
  579.3 238.6 %reduce-scatter.7.cloned.1.call-start = ((), (), s32[]{:S(2)}) async-start(), calls=%async_computation.11 | async-start | bytes 8478720 | tf_op jit(solution)/shard_map/reduce_scatter | solution.py:217
  605.3 232.9 %all-gather.25.cloned.1.call-start = ((), (), s32[]{:S(2)}) async-start(), calls=%async_computation.14 | async-start | bytes 5087232 | tf_op jit(solution)/shard_map/all_gather | solution.py:261
  824.7 221.6 %all-reduce.11.cloned.1.call-start = ((), (), s32[]{:S(2)}) async-start(), calls=%async_computation.17 | async-start | bytes 7077888 | tf_op jit(solution)/shard_map/psum | solution.py:318
  848.2 99.5 %copy-start.20 = (f32[2,729,16]{1,2,0:T(8,128)S(1)}, f32[2,729,16]{1,2,0:T(8,128)}, u32[]{:S(2)}) copy-start(f32[2,729,16]{1,2,0:T(8,128)} %copy-done.19) | copy-start | bytes 279940
  879.1 13.2 copy-start.59
  928.8 13.2 copy-start.59
  960.1 145.3 %all-reduce.15.cloned.1.call-start = ((), (), s32[]{:S(2)}) async-start(), calls=%async_computation.19 | async-start | bytes 1179648 | tf_op jit(solution)/shard_map/psum | solution.py:328
  975.0 250.2 %all-reduce.9.cloned.1.call-start = ((), (), s32[]{:S(2)}) async-start(), calls=%async_computation.16 | async-start | bytes 2621440 | tf_op jit(solution)/shard_map/psum | solution.py:324
  982.6 64.1 %copy-start.58 = (bf16[2,729,8,72]{1,3,2,0:T(8,128)(2,1)S(1)}, bf16[2,729,8,72]{1,3,2,0:T(8,128)(2,1)}, u32[]{:S(2)}) copy-start(bf16[2,729,8,72]{1,3,2,0:T(8,128)(2,1)} %get-tuple-element.96) | copy-start | bytes 5038852
  985.4 337.2 %all-reduce.13.cloned.1.call-start = ((), (), s32[]{:S(2)}) async-start(), calls=%async_computation.18 | async-start | bytes 7077888 | tf_op jit(solution)/shard_map/psum | solution.py:317
  1046.3 289.8 %reduce-scatter.11.cloned.1.call-start = ((), (), s32[]{:S(2)}) async-start(), calls=%async_computation.15 | async-start | bytes 5087232 | tf_op jit(solution)/shard_map/reduce_scatter | solution.py:292
  1322.6 13.5 copy-start.37
  1322.6 13.5 copy-start.40
  1322.6 13.5 copy-start.44
  (57 other events, 309.4 us)
Sparse Core Ops, SparseCore 0:
  18.0 15.1 all-gather.10
  35.0 55.7 all-gather.12
  92.7 30.1 all-gather.14
  177.7 11.1 reduce-scatter.4
  824.8 13.0 all-gather.24
  960.2 85.9 all-reduce.10
  1050.3 55.0 all-reduce.14
  1111.4 113.6 all-reduce.8
  1229.0 93.5 all-reduce.12
  1324.8 11.1 reduce-scatter.10
Sparse Core Ops, SparseCore 1:
  181.1 123.2 all-gather.22
  306.0 37.9 all-gather.20
  345.7 39.7 all-gather.18
  387.1 123.2 all-gather.16
  579.4 116.8 reduce-scatter.8
  698.8 119.1 reduce-scatter.6
